TPU v7x, 32 devices: a whole 2x2x4 slice. The times are simulated.
32 devices in a mesh: row: 4 (over x, core), col: 8 (over z, y).
Axes of the slice: x: 2, y: 2, z: 4, core: 2. Of those that a mesh axis runs over, the one named last changes fastest.
Arguments:
- coords: float32 [4, 4096], P(None, ('row', 'col')), may hold values from 0 to 1, as said below
- values: float32 [512, 4096], P(None, ('row', 'col')), may hold values from -6 to 6
- coarse_coords: float32 [4, 512], P(None, ('row', 'col')), may hold values from 0 to 1, as said below
- coarse_values: float32 [512, 512], P(None, ('row', 'col')), may hold values from -6 to 6
- fine_index: int32 [32, 128], P(('row', 'col')), may hold values from 0 to 127, as said below
- coarse_index: int32 [32, 384], P(('row', 'col')), may hold values from 0 to 511, as said below
- log_params: float32 [6], replicated, may hold values from -0.5 to 0.5
Outputs:
- step: float32 [6], replicated
- whitened: float32 [512, 4096], P(None, ('row', 'col'))
Inputs may be any that keep to these rules, and one draw needn't show every extreme that they name: `fine_index`: in each row the first 64 entries are distinct, and so are the last 64. `coarse_index`: the entries of each row are distinct; in each row at most 16 entries lie in one tile (j // 16), and some tile holds exactly 16 of them. `coarse_coords`: coarse point j lies in tile j // 16; for tile (r, c) its longitude lies in [c / 8, (c + 1) / 8) and its latitude in [r / 4, (r + 1) / 4), elevation and time in [0, 1). `coords`: fine point p lies in tile p // 128, placed as for the coarse points.
All inputs are finite; a program needn't handle non-finite values.
Results may differ from a plain program's by a relative error of at most 0.0003.
Values sent between devices are 32-bit elements; how exact they have to be, the bound alone decides.
A program may use at most 192 MiB of HBM per device.

v0:
```python
import math
import jax
import jax.numpy as jnp
from jax import lax
from jax.sharding import PartitionSpec as P

HIGH = lax.Precision.HIGHEST
ROOT_FIVE = math.sqrt(5.0)
NUGGET = 0.2
RANGE_BASE = (0.5, 0.5, 0.5, 0.5)


def shifted(value, axis, steps):
    count = lax.axis_size(axis)
    first, last = (max(0, -steps), min(count, count - steps))
    return lax.ppermute(value, axis, [(source, source + steps) for source in range(first, last)])


def passed_along(block, axis, distance):
    devices = range(lax.axis_size(axis))
    route = [((i - distance) % len(devices), i) for i in devices]
    return lax.ppermute(block, axis, route)


def local_covariance(joint_coords, live, theta):
    count = joint_coords.shape[1]
    scale = jnp.exp(theta[1:5]) * jnp.array(RANGE_BASE)
    scaled = joint_coords / scale[:, None]
    diff = scaled[:, :, None] - scaled[:, None, :]
    squares = diff * diff
    dist = jnp.sqrt(jnp.sum(squares, axis=0))
    root = ROOT_FIVE * dist
    decay = jnp.exp(-root)
    variance = jnp.exp(theta[0])
    kernel = variance * (1.0 + root + root * root / 3.0) * decay
    common = variance * (5.0 / 3.0) * (1.0 + root) * decay
    paired = live[:, None] * live[None, :]
    ident = jnp.eye(count, dtype=jnp.float32)
    nugget = NUGGET * jnp.exp(theta[5])
    cov = paired * kernel + (live * nugget + 1.0 - live)[:, None] * ident
    derivs = jnp.concatenate(
        [
            (paired * kernel)[None],
            (paired * common)[None] * squares,
            ((live * nugget)[:, None] * ident)[None],
        ],
        axis=0,
    )
    return (cov, derivs)


def fisher_terms(cov, derivs, lead, reps):
    count = cov.shape[0]
    ident = jnp.eye(count, dtype=jnp.float32)
    factor = jnp.linalg.cholesky(cov)
    inverse = jax.scipy.linalg.solve_triangular(factor, ident, lower=True)
    joint_prec = jnp.dot(inverse.T, inverse, precision=HIGH)
    lead_inv = inverse[:lead, :lead]
    lead_prec = jnp.dot(lead_inv.T, lead_inv, precision=HIGH)
    joint_prod = jnp.einsum("ab,ibc->iac", joint_prec, derivs, precision=HIGH)
    lead_prod = jnp.einsum("ab,ibc->iac", lead_prec, derivs[:, :lead, :lead], precision=HIGH)
    joint_fish = jnp.einsum("iab,jba->ij", joint_prod, joint_prod, precision=HIGH)
    lead_fish = jnp.einsum("iab,jba->ij", lead_prod, lead_prod, precision=HIGH)
    fisher = reps * 0.5 * (joint_fish - lead_fish)
    traces = jnp.trace(joint_prod, axis1=1, axis2=2) - jnp.trace(lead_prod, axis1=1, axis2=2)
    return (inverse, fisher, traces)


def score_terms(inverse, derivs, joint_values, traces, lead, reps):
    white = jnp.dot(joint_values, inverse.T, precision=HIGH)
    alpha = jnp.dot(white, inverse, precision=HIGH)
    lead_alpha = jnp.dot(white[:, :lead], inverse[:lead, :lead], precision=HIGH)
    joint_quad = jnp.sum(
        jnp.einsum("rn,inm->irm", alpha, derivs, precision=HIGH) * alpha[None], axis=(1, 2)
    )
    lead_quad = jnp.sum(
        jnp.einsum("rn,inm->irm", lead_alpha, derivs[:, :lead, :lead], precision=HIGH)
        * lead_alpha[None],
        axis=(1, 2),
    )
    grad = 0.5 * (joint_quad - lead_quad) - 0.5 * reps * traces
    return (grad, white[:, lead:])


def body(coords, values, coarse_coords, coarse_values, fine_index, coarse_index, log_params):
    half = fine_index.shape[1] // 2
    reps = values.shape[0]
    block_size = coords.shape[1]
    pick_upper = fine_index[0, :half]
    pick_left = fine_index[0, half:]
    wanted = coarse_index[0]
    num_coarse = wanted.shape[0]
    lead = num_coarse + 2 * half
    upper_coords, upper_values = shifted((coords, values), "row", 1)
    left_coords, left_values = passed_along((coords, values), "col", 1)
    upper_coords = jnp.take(upper_coords, pick_upper, axis=1)
    upper_values = jnp.take(upper_values, pick_upper, axis=1)
    left_coords = jnp.take(left_coords, pick_left, axis=1)
    left_values = jnp.take(left_values, pick_left, axis=1)
    piece_coords = lax.all_gather(coarse_coords, ("row", "col"), axis=1, tiled=True)
    piece_values = lax.all_gather(coarse_values, ("row", "col"), axis=1, tiled=True)
    width = piece_coords.shape[1]
    onehot = (wanted[None, :] == jnp.arange(width, dtype=jnp.int32)[:, None]).astype(jnp.float32)
    picked_coords = jnp.dot(piece_coords, onehot, precision=HIGH)
    picked_values = jnp.dot(piece_values, onehot, precision=HIGH)
    upper_live = (lax.axis_index("row") > 0).astype(jnp.float32)
    joint_coords = jnp.concatenate([picked_coords, upper_coords, left_coords, coords], axis=1)
    joint_values = jnp.concatenate([picked_values, upper_values, left_values, values], axis=1)
    live = jnp.concatenate(
        [
            jnp.ones((num_coarse,), jnp.float32),
            upper_live * jnp.ones((half,), jnp.float32),
            jnp.ones((half + block_size,), jnp.float32),
        ]
    )
    cov, derivs = local_covariance(joint_coords, live, log_params)
    inverse, fisher, traces = fisher_terms(cov, derivs, lead, reps)
    grad, white = score_terms(inverse, derivs, joint_values, traces, lead, reps)
    grad, fisher = lax.psum((grad, fisher), ("row", "col"))
    step = jax.scipy.linalg.cho_solve((jnp.linalg.cholesky(fisher), True), grad)
    return (step, white)


def solution(mesh):
    in_specs = (
        P(None, ("row", "col")),
        P(None, ("row", "col")),
        P(None, ("row", "col")),
        P(None, ("row", "col")),
        P(("row", "col"), None),
        P(("row", "col"), None),
        P(),
    )
    out_specs = (P(), P(None, ("row", "col")))
    return jax.shard_map(body, mesh=mesh, in_specs=in_specs, out_specs=out_specs, check_vma=False)
```

profile of v0, /device:TPU:14, one launch (start us, length us, event | category | flops | bytes accessed | tf_op | source)
XLA Modules:
  0.0 582.0 jit_solution(4296260236476704063)
XLA Ops:
  9.6 1.9 collective-permute-start
  14.8 1.9 collective-permute-start.2
  21.9 61.8 %all-gather = f32[32,16,4]{1,2,0:T(4,128)S(1)} all-gather(f32[1,16,4]{1,2,0:T(4,128)S(1)} %bitcast.157), channel_id=1, replica_groups=mesh['row'=4,'col'=8] {'row','col'}, dimensions={0}, use_global_device_ids=true | all-gather | bytes 8448 | tf_op jit(solution)/shard_map/all_gather | solution.py:100
  90.9 3.2 negate_exponential_fusion
  95.2 2.1 copy.63
  100.1 2.7 copy.66
  102.8 3.2 copy.65
  106.0 2.3 add_multiply_fusion.1
  109.5 11.7 %cholesky.146 = f32[128,128]{1,0:T(8,128)S(1)} custom-call(f32[128,128]{1,0:T(8,128)S(1)} %cholesky.372), custom_call_target="Cholesky" | custom-call | tf_op jit(solution)/shard_map/jit(cholesky)/cholesky | solution.py:55
  123.4 11.3 %custom-call.49 = f32[1,128,128]{1,2,0:T(8,128)} custom-call(f32[1,128,128]{2,1,0:T(8,128)} %get-tuple-element.43), custom_call_target="InvertDiagBlocksLowerTriangular" | custom-call | tf_op jit(solution)/shard_map/jit(cholesky)/cholesky | solution.py:55
  137.7 13.2 %cholesky.171 = f32[128,128]{1,0:T(8,128)} custom-call(f32[128,128]{1,0:T(8,128)} %cholesky.376), custom_call_target="Cholesky" | custom-call | tf_op jit(solution)/shard_map/jit(cholesky)/cholesky | solution.py:55
  150.8 2.0 select_reduce_fusion.5
  152.9 11.4 %custom-call.50 = f32[1,128,128]{1,2,0:T(8,128)} custom-call(f32[1,128,128]{2,1,0:T(8,128)} %get-tuple-element.40), custom_call_target="InvertDiagBlocksLowerTriangular" | custom-call | tf_op jit(solution)/shard_map/jit(cholesky)/cholesky | solution.py:55
  167.3 13.2 %cholesky.317 = f32[128,128]{1,0:T(8,128)} custom-call(f32[128,128]{1,0:T(8,128)} %cholesky.381), custom_call_target="Cholesky" | custom-call | tf_op jit(solution)/shard_map/jit(cholesky)/cholesky | solution.py:55
  180.5 2.0 select_reduce_fusion.4
  182.5 11.3 %custom-call.51 = f32[1,128,128]{1,2,0:T(8,128)} custom-call(f32[1,128,128]{2,1,0:T(8,128)} %get-tuple-element.37), custom_call_target="InvertDiagBlocksLowerTriangular" | custom-call | tf_op jit(solution)/shard_map/jit(cholesky)/cholesky | solution.py:55
  196.7 13.4 %cholesky.336 = f32[128,128]{1,0:T(8,128)} custom-call(f32[128,128]{1,0:T(8,128)} %cholesky.386), custom_call_target="Cholesky" | custom-call | tf_op jit(solution)/shard_map/jit(cholesky)/cholesky | solution.py:55
  210.0 2.1 select_reduce_fusion.3
  212.1 11.3 %custom-call.52 = f32[1,128,128]{1,2,0:T(8,128)} custom-call(f32[1,128,128]{2,1,0:T(8,128)} %get-tuple-element.34), custom_call_target="InvertDiagBlocksLowerTriangular" | custom-call | tf_op jit(solution)/shard_map/jit(cholesky)/cholesky | solution.py:55
  225.4 12.5 %cholesky.353 = f32[128,128]{1,0:T(8,128)S(1)} custom-call(f32[128,128]{1,0:T(8,128)} %convolution_subtract_fusion.6), custom_call_target="Cholesky" | custom-call | tf_op jit(solution)/shard_map/jit(cholesky)/cholesky | solution.py:55
  247.0 13.1 %while.1 = (s32[]{:T(128)}, f32[640,640]{1,0:T(8,128)S(1)}, s32[5,2]{0,1:T(2,128)S(1)}, f32[5,128,128]{2,1,0:T(8,128)}, s32[]{:T(128)}) while((s32[]{:T(128)}, f32[640,640]{1,0:T(8,128)S(1)}, s32[5,2]{0,1:T(2,128)S(1)}, f32[5,128,128]{2,1,0:T(8,128)}, s32[]{:T(128)}) %tuple.51), condition=%wide.while_cond, body=%wide.while_body.sunk | while | flops 2 | bytes 132205 | solution.py:56
  247.6 2.0 bitcast_dynamic-update-slice_fusion.2
  250.3 2.0 bitcast_dynamic-update-slice_fusion.2
  252.9 2.0 bitcast_dynamic-update-slice_fusion.2
  255.5 2.0 bitcast_dynamic-update-slice_fusion.2
  258.1 2.0 bitcast_dynamic-update-slice_fusion.2
  261.3 50.9 %custom-call.53 = f32[5,128,128]{1,2,0:T(8,128)} custom-call(f32[5,128,128]{2,1,0:T(8,128)} %get-tuple-element.11), custom_call_target="InvertDiagBlocksLowerTriangular" | custom-call | tf_op jit(solution)/shard_map/jit(_solve_triangular)/triangular_solve | solution.py:56
  318.3 1.9 convolution_subtract_fusion.2
  320.7 2.0 fusion.30
  322.7 2.9 convolution_bitcast_fusion.1
  326.1 6.2 %fusion.100 = f32[640,640]{1,0:T(8,128)} fusion(f32[640,640]{1,0:T(8,128)S(1)} %convolution_dynamic-update-slice_fusion), kind=kOutput, calls=%fused_computation.189 | convolution fusion | flops 3145728000 | bytes 3276800 | tf_op jit(solution)/shard_map/dot_general | solution.py:57
  332.4 3.8 fusion.7
  336.2 2.9 copy.64
  339.0 30.9 %select_reduce_fusion = (f32[6]{0:T(128)S(1)}, f32[6,640,640]{1,2,0:T(8,128)}) fusion(pred[640,640]{0,1:T(8,128)(4,1)S(1)} %copy-done.22, f32[640,640]{1,0:T(8,128)} %fusion.100, f32[1,640,640]{1,2,0:T(8,128)S(1)} %copy-done.4, f32[4,640,640]{1,2,0:T(8,128)} %fusion.7, f32[1,640,640]{1,2,0:T(8,128)} %copy.64), kind=kOutput, calls=%fused_computation.9 | convolution fusion | flops 18884198400 | bytes 21708824 | tf_op jit(solution)/shard_map/ab,ibc->iac/dot_general | solution.py:60
  369.9 14.5 %copy.67 = f32[6,640,640]{2,0,1:T(8,128)} copy(f32[6,640,640]{1,2,0:T(8,128)} %get-tuple-element.63) | data formatting | bytes 19660800 | tf_op jit(solution)/shard_map/ab,ibc->iac/transpose | solution.py:60
  384.4 16.0 %select_reduce_fusion.1 = (f32[6]{0:T(128)S(1)}, f32[6,512,512]{1,2,0:T(8,128)}) fusion(pred[512,512]{0,1:T(8,128)(4,1)S(1)} %copy-done.17, f32[512,512,1]{1,0,2:T(8,128)S(1)} %copy-done.18, f32[1,640,640]{1,2,0:T(8,128)S(1)} %copy-done.4, f32[4,640,640]{1,2,0:T(8,128)} %fusion.7, f32[1,640,640]{1,2,0:T(8,128)} %copy.64), kind=kOutput, calls=%fused_computation.22 | convolution fusion | flops 9669967872 | bytes 17432600 | tf_op jit(solution)/shard_map/ab,ibc->iac/dot_general | solution.py:61
  400.4 9.8 %copy.69 = f32[6,512,512]{2,0,1:T(8,128)} copy(f32[6,512,512]{1,2,0:T(8,128)} %get-tuple-element.65) | data formatting | bytes 12582912 | tf_op jit(solution)/shard_map/ab,ibc->iac/transpose | solution.py:61
  410.2 34.7 %fusion.36 = f32[6,6]{0,1:T(8,128)S(1)} fusion(f32[6,640,640]{2,0,1:T(8,128)} %copy.67, f32[6,640,640]{1,2,0:T(8,128)} %get-tuple-element.63), kind=kOutput, calls=%fused_computation.72 | convolution fusion | flops 176947200 | bytes 19660944 | tf_op jit(solution)/shard_map/iab,jba->ij/dot_general | solution.py:62
  445.0 18.9 %fusion.42 = f32[6,6]{0,1:T(8,128)S(1)} fusion(f32[6,6]{0,1:T(8,128)S(1)} %fusion.36, f32[6,512,512]{2,0,1:T(8,128)S(1)} %copy-done, f32[6,512,512]{1,2,0:T(8,128)S(1)} %bitcast.156), kind=kOutput, calls=%fused_computation.74 | convolution fusion | flops 113246280 | bytes 12583200 | tf_op jit(solution)/shard_map/iab,jba->ij/dot_general | solution.py:63
  466.8 2.3 convolution_bitcast_fusion.2
  469.0 7.4 %fusion.21 = f32[512,640]{1,0:T(8,128)S(1)} fusion(f32[640,640]{1,0:T(8,128)S(1)} %copy-done.2, f32[512,128]{0,1:T(8,128)} %copy.75, f32[512,64]{0,1:T(8,128)S(1)} %select_bitcast_fusion, f32[512,64]{0,1:T(8,128)S(1)} %select_bitcast_fusion.1, f32[512,384]{0,1:T(8,128)S(1)} %convolution_bitcast_fusion.2), kind=kOutput, calls=%fused_computation.48 | convolution fusion | flops 2517565440 | bytes 4259840 | tf_op jit(solution)/shard_map/dot_general | solution.py:70
  476.5 4.8 fusion.101
  481.3 3.0 fusion.45
  484.3 2.9 copy.78
  487.2 21.7 %fusion.4 = f32[6]{0:T(128)S(1)} fusion(f32[512,640]{0,1:T(8,128)} %copy.78, f32[1,640,640]{1,2,0:T(8,128)S(1)} %copy-done.5, f32[4,640,640]{1,2,0:T(8,128)} %fusion.7, f32[1,640,640]{1,2,0:T(8,128)} %copy.64, f32[512,640]{1,0:T(8,128)} %fusion.101), kind=kOutput, calls=%fused_computation.13 | convolution fusion | flops 15108341760 | bytes 12451864 | tf_op jit(solution)/shard_map/rn,inm->irm/dot_general | solution.py:74
  508.9 2.6 copy.79
  511.5 14.1 %fusion.9 = f32[6]{0:T(128)S(1)} fusion(f32[512,512]{0,1:T(8,128)} %copy.79, f32[1,640,640]{1,2,0:T(8,128)S(1)} %copy-done.5, f32[4,640,640]{1,2,0:T(8,128)} %fusion.7, f32[1,640,640]{1,2,0:T(8,128)} %copy.64, f32[512,512]{1,0:T(8,128)} %fusion.45), kind=kOutput, calls=%fused_computation.21 | convolution fusion | flops 9669967872 | bytes 11927576 | tf_op jit(solution)/shard_map/rn,inm->irm/dot_general | solution.py:77
  526.3 45.2 %all-reduce.1 = (f32[6,6]{0,1:T(8,128)S(1)}, f32[6]{0:T(128)S(1)}) all-reduce(f32[6,6]{0,1:T(8,128)S(1)} %fusion.42, f32[6]{0:T(128)S(1)} %multiply_subtract_fusion), channel_id=1, replica_groups=mesh['row'=4,'col'=8] {'row','col'}, use_global_device_ids=true, to_apply=%region_11.13 | all-reduce | flops 42 | bytes 336 | tf_op jit(solution)/shard_map/psum | solution.py:119
  (178 shorter events, 58.6 us)
Async XLA Ops:
  7.2 14.6 %copy-start.36 = (s32[1,128]{1,0:T(1,128)S(1)}, s32[1,128]{1,0:T(1,128)}, u32[]{:S(2)}) copy-start(s32[1,128]{1,0:T(1,128)} %param.16) | copy-start | bytes 1540
  7.2 14.7 %copy-start.35 = (f32[4,16]{1,0:T(4,128)S(1)}, f32[4,16]{1,0:T(4,128)}, u32[]{:S(2)}) copy-start(f32[4,16]{1,0:T(4,128)} %param.14) | copy-start | bytes 772
  7.2 76.6 %copy-start.37 = (s32[1,384]{1,0:T(1,128)S(1)}, s32[1,384]{1,0:T(1,128)}, u32[]{:S(2)}) copy-start(s32[1,384]{1,0:T(1,128)} %param.17) | copy-start | bytes 4612
  7.2 459.5 %all-gather.3.cloned.1.call-start = ((), (), s32[]{:S(2)}) async-start(), calls=%async_computation | async-start | bytes 1081344 | tf_op jit(solution)/shard_map/all_gather | solution.py:101
  8.0 80.7 %collective-permute-start.1 = (f32[4,128]{0,1:T(8,128)S(1)}, f32[4,128]{0,1:T(8,128)S(1)}, u32[]{:S(2)}, u32[]{:S(2)}) collective-permute-start(f32[4,128]{0,1:T(8,128)S(1)} %copy.58), channel_id=1, source_target_pairs={{7,0},{0,1},{1,2},{2,3},{3,4},{4,5},{5,6},{6,7},{15,8},{8,9},{9,10... | collective-permute-start | bytes 6152 | tf_op jit(solution)/shard_map/ppermute | solution.py:22
  9.6 79.8 %collective-permute-start = (f32[4,128]{0,1:T(8,128)S(1)}, f32[4,128]{0,1:T(8,128)S(1)}, u32[]{:S(2)}, u32[]{:S(2)}) collective-permute-start(f32[4,128]{0,1:T(8,128)S(1)} %copy.58), channel_id=1, source_target_pairs={{0,8},{8,16},{16,24},{1,9},{9,17},{17,25},{2,10},{10,18},{18,26},{... | collective-permute-start | bytes 6152 | tf_op jit(solution)/shard_map/ppermute | solution.py:16
  13.3 450.6 %collective-permute-start.3 = (f32[512,128]{0,1:T(8,128)}, f32[512,128]{0,1:T(8,128)}, u32[]{:S(2)}, u32[]{:S(2)}) collective-permute-start(f32[512,128]{0,1:T(8,128)} %copy.75), channel_id=1, source_target_pairs={{7,0},{0,1},{1,2},{2,3},{3,4},{4,5},{5,6},{6,7},{15,8},{8,9},{9,10... | collective-permute-start | bytes 786440 | tf_op jit(solution)/shard_map/ppermute | solution.py:22
  14.8 450.9 %collective-permute-start.2 = (f32[512,128]{0,1:T(8,128)}, f32[512,128]{0,1:T(8,128)S(1)}, u32[]{:S(2)}, u32[]{:S(2)}) collective-permute-start(f32[512,128]{0,1:T(8,128)} %copy.75), channel_id=1, source_target_pairs={{0,8},{8,16},{16,24},{1,9},{9,17},{17,25},{2,10},{10,18},{18,26},{... | collective-permute-start | bytes 786440 | tf_op jit(solution)/shard_map/ppermute | solution.py:16
  16.9 69.8 %copy-start.14 = (pred[640,640]{1,0:T(32,128)(4,1)}, pred[640,640]{1,0:T(32,128)(4,1)S(1)}, u32[]{:S(2)}) copy-start(pred[640,640]{1,0:T(32,128)(4,1)S(1)} %iota_compare_fusion.1) | copy-start | bytes 1228804
  20.3 69.8 %copy-start.26 = (f32[4,128]{1,0:T(4,128)S(1)}, f32[4,128]{1,0:T(4,128)}, u32[]{:S(2)}) copy-start(f32[4,128]{1,0:T(4,128)} %param.12) | copy-start | bytes 6148
  21.8 69.0 %copy-start.31 = (pred[64]{0:T(512)(128)(4,1)}, pred[64]{0:T(512)(128)(4,1)S(1)}, u32[]{:S(2)}) copy-start(pred[64]{0:T(512)(128)(4,1)S(1)} %get-tuple-element.22) | copy-start | bytes 196
  21.8 69.0 %copy-start.33 = (pred[64]{0:T(512)(128)(4,1)}, pred[64]{0:T(512)(128)(4,1)S(1)}, u32[]{:S(2)}) copy-start(pred[64]{0:T(512)(128)(4,1)S(1)} %get-tuple-element.50) | copy-start | bytes 196
  21.8 68.2 %copy-start.30 = (s32[1024]{0:T(1024)}, s32[1024]{0:T(1024)S(1)}, u32[]{:S(2)}) copy-start(s32[1024]{0:T(1024)S(1)} %pad_clamp_fusion) | copy-start | bytes 12292
  21.9 68.2 %copy-start.29 = (s32[1024]{0:T(1024)}, s32[1024]{0:T(1024)S(1)}, u32[]{:S(2)}) copy-start(s32[1024]{0:T(1024)S(1)} %pad_clamp_fusion.1) | copy-start | bytes 12292
  83.8 7.1 %copy-start.27 = (s32[384]{0:T(512)}, s32[384]{0:T(512)S(1)}, u32[]{:S(2)}) copy-start(s32[384]{0:T(512)S(1)} %reduce.36) | copy-start | bytes 4612
  102.8 3.2 copy-start.25
  108.4 1.2 copy-start.9
  109.5 25.2 %copy-start.10 = (f32[640,640]{1,0:T(8,128)S(1)}, f32[640,640]{1,0:T(8,128)}, u32[]{:S(2)}) copy-start(f32[640,640]{1,0:T(8,128)} %copy-done.9) | copy-start | bytes 4915204
  121.2 0.6 copy-start.24
  136.3 0.7 copy-start.19
  166.0 0.7 copy-start.20
  195.4 0.7 copy-start.21
  246.3 0.7 copy-start.38
  260.1 1.2 copy-start.11
  260.1 56.1 %copy-start.8 = (f32[640,640]{1,0:T(8,128)S(1)}, f32[640,640]{1,0:T(8,128)}, u32[]{:S(2)}) copy-start(f32[640,640]{1,0:T(8,128)} %fusion.53) | copy-start | bytes 4915204
  313.4 4.4 copy-start.23
  316.2 6.5 %copy-start.6 = (f32[128,640]{1,0:T(8,128)}, f32[128,640]{1,0:T(8,128)S(1)}, u32[]{:S(2)}) copy-start(f32[128,640]{1,0:T(8,128)S(1)} %get-tuple-element.57) | copy-start | bytes 983044
  318.3 4.4 copy-start.12
  320.7 5.0 copy-start.15
  326.1 6.2 %copy-start.1 = (f32[640,640]{1,0:T(8,128)}, f32[640,640]{1,0:T(8,128)S(1)}, u32[]{:S(2)}) copy-start(f32[640,640]{1,0:T(8,128)S(1)} %convolution_dynamic-update-slice_fusion) | copy-start | bytes 4915204
  326.1 6.2 %copy-start.3 = (f32[640,640]{0,1:T(8,128)S(1)}, f32[640,640]{0,1:T(8,128)}, u32[]{:S(2)}) copy-start(f32[640,640]{0,1:T(8,128)} %get-tuple-element.30) | copy-start | bytes 4915204
  336.1 2.9 copy-start.4
  336.1 2.9 copy-start.22
  369.9 14.5 %copy-start.17 = (pred[512,512]{0,1:T(8,128)(4,1)S(1)}, pred[512,512]{0,1:T(8,128)(4,1)}, u32[]{:S(2)}) copy-start(pred[512,512]{0,1:T(8,128)(4,1)} %iota_compare_fusion.4) | copy-start | bytes 786436
  369.9 14.5 %copy-start.18 = (f32[512,512,1]{1,0,2:T(8,128)S(1)}, f32[512,512,1]{1,0,2:T(8,128)}, u32[]{:S(2)}) copy-start(f32[512,512,1]{1,0,2:T(8,128)} %convolution_bitcast_fusion.1) | copy-start | bytes 3145732
  400.4 44.5 %slice-start = ((s8[6291456]{0:T(1024)(128)(4,1)}), s8[2097152]{0:T(1024)(128)(4,1)S(1)}, s32[]{:S(2)}) async-start(s8[6291456]{0:T(1024)(128)(4,1)} %bitcast.155), calls=%async_computation.1 | async-start | bytes 4194304
  410.2 34.8 %slice-start.1 = ((s8[6291456]{0:T(1024)(128)(4,1)}), s8[4194304]{0:T(1024)(128)(4,1)S(1)}, s32[]{:S(2)}) async-start(s8[6291456]{0:T(1024)(128)(4,1)} %bitcast.155), calls=%async_computation.2 | async-start | bytes 8388608
  410.2 34.8 %copy-start = (f32[6,512,512]{2,0,1:T(8,128)S(1)}, f32[6,512,512]{2,0,1:T(8,128)}, u32[]{:S(2)}) copy-start(f32[6,512,512]{2,0,1:T(8,128)} %copy.69) | copy-start | bytes 18874372
  465.7 0.8 copy-start.34
  465.7 0.9 copy-start.32
  465.7 1.0 copy-start.28
  466.5 2.5 copy-start.2
  476.5 4.8 copy-start.7
  476.5 4.8 copy-start.13
  476.5 4.8 copy-start.16
  484.3 2.9 copy-start.5
Sparse Core Ops, SparseCore 0:
  16.9 53.3 all-gather.2
where the time goes:
time: 589 us; the launch traced here: 582 us
  other arithmetic  193 us (33%)
  matrix products  182 us (31%)
  blocking collectives  107 us (18%)
  local copies, waits for them, and re-layouts  73.2 us (12%)
  between operations  19.7 us (3%)
  starting transfers between devices  6.94 us (1%)
    another operation x19, other arithmetic, fisher_terms(): factor = jnp.linalg.cholesky(cov)  121 us
    all_gather x1, blocking collectives, body(): lax.all_gather(coarse_coords, ('row', 'col'), axis=1, tiled=True)  61.8 us
    another operation x3, other arithmetic, fisher_terms(): inverse = jax.scipy.linalg.solve_triangular(factor, ident, lower=True)  51.7 us
    psum x1, blocking collectives, body(): grad, fisher = lax.psum((grad, fisher), ('row', 'col'))  45.2 us
    dot_general x1, matrix products, fisher_terms(): jnp.einsum('iab,jba->ij', joint_prod, joint_prod, precision=HIGH)  34.7 us
    dot_general x1, matrix products, fisher_terms(): joint_prod = jnp.einsum('ab,ibc->iac', joint_prec, derivs, precision=HIGH)  30.9 us
    dot_general x1, matrix products, score_terms(): jnp.einsum('rn,inm->irm', alpha, derivs, precision=HIGH) * alpha[None]  21.7 us
    dot_general x1, matrix products, fisher_terms(): lead_fish = jnp.einsum('iab,jba->ij', lead_prod, lead_prod, precision=HIGH)  18.9 us
  transfers between devices with their start and end apart: 5, of which 0 were waited for; matrix products, arithmetic and copies ran while one was open for 65% of the time, Pallas kernels for 0%

commit v1 on v0

--- a/solution.py
+++ b/solution.py
@@ -97,7 +97,22 @@
     upper_values = jnp.take(upper_values, pick_upper, axis=1)
     left_coords = jnp.take(left_coords, pick_left, axis=1)
     left_values = jnp.take(left_values, pick_left, axis=1)
-    piece_coords = lax.all_gather(coarse_coords, ("row", "col"), axis=1, tiled=True)
+    ways, here, turn = (
+        lax.axis_size(("row", "col")),
+        lax.axis_index(("row", "col")),
+        coarse_coords.shape[1],
+    )
+    line, have = (coarse_coords, 1)
+    while have < ways:
+        line = jnp.concatenate(
+            [
+                line,
+                lax.ppermute(line, ("row", "col"), [(d, (d - have) % ways) for d in range(ways)]),
+            ],
+            axis=1,
+        )
+        have = 2 * have
+    piece_coords = jnp.roll(line, here * turn, axis=1)
     piece_values = lax.all_gather(coarse_values, ("row", "col"), axis=1, tiled=True)
     width = piece_coords.shape[1]
     onehot = (wanted[None, :] == jnp.arange(width, dtype=jnp.int32)[:, None]).astype(jnp.float32)

time: 589 us -> 540 us (0.917)
  blocking collectives: 107 us -> 43.9 us
  waiting for transfers between devices: 0.05 us -> 6.74 us
  starting transfers between devices: 6.94 us -> 13 us
    all_gather x1 -> x0, blocking collectives: 61.8 us -> none  [body(): lax.all_gather(coarse_coords, ('row', 'col'), axis=1, tiled=True)]
    ppermute x0 -> x5, waiting for transfers between devices: none -> 6.69 us  [body(): lax.ppermute(line, ('row', 'col'), [(d, (d - have) % ways) for d in range...]
    ppermute x0 -> x5, starting transfers between devices: none -> 6.05 us  [body(): lax.ppermute(line, ('row', 'col'), [(d, (d - have) % ways) for d in range...]
  transfers between devices with their start and end apart: 5 -> 10, of which waited for: 0 -> 3; matrix products, arithmetic and copies ran while one was open for 65% -> 71% of each run, Pallas kernels for 0% -> 0%
where the time goes in v1:
time: 540 us; the launch traced here: 533 us
  other arithmetic  193 us (36%)
  matrix products  182 us (34%)
  local copies, waits for them, and re-layouts  73.9 us (14%)
  blocking collectives  43.9 us (8%)
  between operations  19.7 us (4%)
  starting transfers between devices  13 us (2%)
  waiting for transfers between devices  6.74 us (1%)
    another operation x19, other arithmetic, fisher_terms(): factor = jnp.linalg.cholesky(cov)  121 us
    another operation x3, other arithmetic, fisher_terms(): inverse = jax.scipy.linalg.solve_triangular(factor, ident, lower=True)  51.6 us
    psum x1, blocking collectives, body(): grad, fisher = lax.psum((grad, fisher), ('row', 'col'))  43.9 us
    dot_general x1, matrix products, fisher_terms(): jnp.einsum('iab,jba->ij', joint_prod, joint_prod, precision=HIGH)  34.7 us
    dot_general x1, matrix products, fisher_terms(): joint_prod = jnp.einsum('ab,ibc->iac', joint_prec, derivs, precision=HIGH)  30.9 us
    dot_general x1, matrix products, score_terms(): jnp.einsum('rn,inm->irm', alpha, derivs, precision=HIGH) * alpha[None]  21.7 us
    dot_general x1, matrix products, fisher_terms(): lead_fish = jnp.einsum('iab,jba->ij', lead_prod, lead_prod, precision=HIGH)  18.9 us
    dot_general x1, matrix products, fisher_terms(): jnp.einsum('ab,ibc->iac', lead_prec, derivs[:, :lead, :lead], precision=H...  16 us
  transfers between devices with their start and end apart: 10, of which 3 were waited for; matrix products, arithmetic and copies ran while one was open for 71% of the time, Pallas kernels for 0%

profile of v1, /device:TPU:14, one launch (start us, length us, event | category | flops | bytes accessed | tf_op | source)
XLA Modules:
  0.0 532.6 jit_solution(16009305162597757081)
XLA Ops:
  24.9 3.1 collective-permute-done.1
  28.1 4.2 collective-permute-start.2
  38.0 2.8 collective-permute-done.4
  42.1 3.3 negate_exponential_fusion
  46.5 2.1 copy.38
  51.4 2.7 copy.41
  54.1 3.2 copy.40
  57.3 2.3 add_multiply_fusion.1
  60.8 11.7 %cholesky.146 = f32[128,128]{1,0:T(8,128)S(1)} custom-call(f32[128,128]{1,0:T(8,128)S(1)} %cholesky.372), custom_call_target="Cholesky" | custom-call | tf_op jit(solution)/shard_map/jit(cholesky)/cholesky | solution.py:55
  74.8 11.3 %custom-call.49 = f32[1,128,128]{1,2,0:T(8,128)} custom-call(f32[1,128,128]{2,1,0:T(8,128)} %get-tuple-element.43), custom_call_target="InvertDiagBlocksLowerTriangular" | custom-call | tf_op jit(solution)/shard_map/jit(cholesky)/cholesky | solution.py:55
  89.0 13.2 %cholesky.171 = f32[128,128]{1,0:T(8,128)} custom-call(f32[128,128]{1,0:T(8,128)} %cholesky.376), custom_call_target="Cholesky" | custom-call | tf_op jit(solution)/shard_map/jit(cholesky)/cholesky | solution.py:55
  102.2 2.0 select_reduce_fusion.5
  104.2 11.4 %custom-call.50 = f32[1,128,128]{1,2,0:T(8,128)} custom-call(f32[1,128,128]{2,1,0:T(8,128)} %get-tuple-element.40), custom_call_target="InvertDiagBlocksLowerTriangular" | custom-call | tf_op jit(solution)/shard_map/jit(cholesky)/cholesky | solution.py:55
  118.6 13.2 %cholesky.317 = f32[128,128]{1,0:T(8,128)} custom-call(f32[128,128]{1,0:T(8,128)} %cholesky.381), custom_call_target="Cholesky" | custom-call | tf_op jit(solution)/shard_map/jit(cholesky)/cholesky | solution.py:55
  131.8 2.0 select_reduce_fusion.4
  133.9 11.3 %custom-call.51 = f32[1,128,128]{1,2,0:T(8,128)} custom-call(f32[1,128,128]{2,1,0:T(8,128)} %get-tuple-element.37), custom_call_target="InvertDiagBlocksLowerTriangular" | custom-call | tf_op jit(solution)/shard_map/jit(cholesky)/cholesky | solution.py:55
  148.1 13.4 %cholesky.336 = f32[128,128]{1,0:T(8,128)} custom-call(f32[128,128]{1,0:T(8,128)} %cholesky.386), custom_call_target="Cholesky" | custom-call | tf_op jit(solution)/shard_map/jit(cholesky)/cholesky | solution.py:55
  161.4 2.0 select_reduce_fusion.3
  163.4 11.3 %custom-call.52 = f32[1,128,128]{1,2,0:T(8,128)} custom-call(f32[1,128,128]{2,1,0:T(8,128)} %get-tuple-element.34), custom_call_target="InvertDiagBlocksLowerTriangular" | custom-call | tf_op jit(solution)/shard_map/jit(cholesky)/cholesky | solution.py:55
  176.8 12.5 %cholesky.353 = f32[128,128]{1,0:T(8,128)S(1)} custom-call(f32[128,128]{1,0:T(8,128)} %convolution_subtract_fusion.6), custom_call_target="Cholesky" | custom-call | tf_op jit(solution)/shard_map/jit(cholesky)/cholesky | solution.py:55
  198.3 13.6 %while.1 = (s32[]{:T(128)}, f32[640,640]{1,0:T(8,128)S(1)}, s32[5,2]{0,1:T(2,128)S(1)}, f32[5,128,128]{2,1,0:T(8,128)}, s32[]{:T(128)}) while((s32[]{:T(128)}, f32[640,640]{1,0:T(8,128)S(1)}, s32[5,2]{0,1:T(2,128)S(1)}, f32[5,128,128]{2,1,0:T(8,128)}, s32[]{:T(128)}) %tuple.51), condition=%wide.while_cond, body=%wide.while_body.sunk | while | flops 2 | bytes 132205 | solution.py:56
  199.0 2.1 bitcast_dynamic-update-slice_fusion.2
  201.7 2.0 bitcast_dynamic-update-slice_fusion.2
  204.4 2.1 bitcast_dynamic-update-slice_fusion.2
  207.2 2.1 bitcast_dynamic-update-slice_fusion.2
  209.9 2.0 bitcast_dynamic-update-slice_fusion.2
  213.1 50.9 %custom-call.53 = f32[5,128,128]{1,2,0:T(8,128)} custom-call(f32[5,128,128]{2,1,0:T(8,128)} %get-tuple-element.11), custom_call_target="InvertDiagBlocksLowerTriangular" | custom-call | tf_op jit(solution)/shard_map/jit(_solve_triangular)/triangular_solve | solution.py:56
  270.1 1.9 convolution_subtract_fusion.2
  272.5 2.0 fusion.30
  274.6 2.9 convolution_bitcast_fusion.1
  277.9 6.2 %fusion.103 = f32[640,640]{1,0:T(8,128)} fusion(f32[640,640]{1,0:T(8,128)S(1)} %convolution_dynamic-update-slice_fusion), kind=kOutput, calls=%fused_computation.194 | convolution fusion | flops 3145728000 | bytes 3276800 | tf_op jit(solution)/shard_map/dot_general | solution.py:57
  284.2 3.8 fusion.7
  288.0 2.9 copy.39
  290.9 30.9 %select_reduce_fusion = (f32[6]{0:T(128)S(1)}, f32[6,640,640]{1,2,0:T(8,128)}) fusion(pred[640,640]{0,1:T(8,128)(4,1)S(1)} %copy-done.22, f32[640,640]{1,0:T(8,128)} %fusion.103, f32[1,640,640]{1,2,0:T(8,128)S(1)} %copy-done.4, f32[4,640,640]{1,2,0:T(8,128)} %fusion.7, f32[1,640,640]{1,2,0:T(8,128)} %copy.39), kind=kOutput, calls=%fused_computation.9 | convolution fusion | flops 18884198400 | bytes 21708824 | tf_op jit(solution)/shard_map/ab,ibc->iac/dot_general | solution.py:60
  321.8 14.5 %copy.42 = f32[6,640,640]{2,0,1:T(8,128)} copy(f32[6,640,640]{1,2,0:T(8,128)} %get-tuple-element.63) | data formatting | bytes 19660800 | tf_op jit(solution)/shard_map/ab,ibc->iac/transpose | solution.py:60
  336.3 16.0 %select_reduce_fusion.1 = (f32[6]{0:T(128)S(1)}, f32[6,512,512]{1,2,0:T(8,128)}) fusion(pred[512,512]{0,1:T(8,128)(4,1)S(1)} %copy-done.17, f32[512,512,1]{1,0,2:T(8,128)S(1)} %copy-done.18, f32[1,640,640]{1,2,0:T(8,128)S(1)} %copy-done.4, f32[4,640,640]{1,2,0:T(8,128)} %fusion.7, f32[1,640,640]{1,2,0:T(8,128)} %copy.39), kind=kOutput, calls=%fused_computation.22 | convolution fusion | flops 9669967872 | bytes 17432600 | tf_op jit(solution)/shard_map/ab,ibc->iac/dot_general | solution.py:61
  352.3 9.7 %copy.44 = f32[6,512,512]{2,0,1:T(8,128)} copy(f32[6,512,512]{1,2,0:T(8,128)} %get-tuple-element.65) | data formatting | bytes 12582912 | tf_op jit(solution)/shard_map/ab,ibc->iac/transpose | solution.py:61
  362.0 34.7 %fusion.36 = f32[6,6]{0,1:T(8,128)S(1)} fusion(f32[6,640,640]{2,0,1:T(8,128)} %copy.42, f32[6,640,640]{1,2,0:T(8,128)} %get-tuple-element.63), kind=kOutput, calls=%fused_computation.71 | convolution fusion | flops 176947200 | bytes 19660944 | tf_op jit(solution)/shard_map/iab,jba->ij/dot_general | solution.py:62
  396.8 18.9 %fusion.42 = f32[6,6]{0,1:T(8,128)S(1)} fusion(f32[6,6]{0,1:T(8,128)S(1)} %fusion.36, f32[6,512,512]{2,0,1:T(8,128)S(1)} %copy-done, f32[6,512,512]{1,2,0:T(8,128)S(1)} %bitcast.148), kind=kOutput, calls=%fused_computation.73 | convolution fusion | flops 113246280 | bytes 12583200 | tf_op jit(solution)/shard_map/iab,jba->ij/dot_general | solution.py:63
  418.6 2.3 convolution_bitcast_fusion.2
  420.9 7.4 %fusion.21 = f32[512,640]{1,0:T(8,128)S(1)} fusion(f32[640,640]{1,0:T(8,128)S(1)} %copy-done.2, f32[512,128]{0,1:T(8,128)} %copy.50, f32[512,64]{0,1:T(8,128)S(1)} %select_bitcast_fusion, f32[512,64]{0,1:T(8,128)S(1)} %select_bitcast_fusion.1, f32[512,384]{0,1:T(8,128)S(1)} %convolution_bitcast_fusion.2), kind=kOutput, calls=%fused_computation.48 | convolution fusion | flops 2517565440 | bytes 4259840 | tf_op jit(solution)/shard_map/dot_general | solution.py:70
  428.3 4.8 fusion.104
  433.1 3.1 fusion.45
  436.2 2.9 copy.53
  439.1 21.7 %fusion.4 = f32[6]{0:T(128)S(1)} fusion(f32[512,640]{0,1:T(8,128)} %copy.53, f32[1,640,640]{1,2,0:T(8,128)S(1)} %copy-done.5, f32[4,640,640]{1,2,0:T(8,128)} %fusion.7, f32[1,640,640]{1,2,0:T(8,128)} %copy.39, f32[512,640]{1,0:T(8,128)} %fusion.104), kind=kOutput, calls=%fused_computation.13 | convolution fusion | flops 15108341760 | bytes 12451864 | tf_op jit(solution)/shard_map/rn,inm->irm/dot_general | solution.py:74
  460.8 2.6 copy.54
  463.4 14.1 %fusion.9 = f32[6]{0:T(128)S(1)} fusion(f32[512,512]{0,1:T(8,128)} %copy.54, f32[1,640,640]{1,2,0:T(8,128)S(1)} %copy-done.5, f32[4,640,640]{1,2,0:T(8,128)} %fusion.7, f32[1,640,640]{1,2,0:T(8,128)} %copy.39, f32[512,512]{1,0:T(8,128)} %fusion.45), kind=kOutput, calls=%fused_computation.21 | convolution fusion | flops 9669967872 | bytes 11927576 | tf_op jit(solution)/shard_map/rn,inm->irm/dot_general | solution.py:77
  478.2 43.9 %all-reduce.1 = (f32[6,6]{0,1:T(8,128)S(1)}, f32[6]{0:T(128)S(1)}) all-reduce(f32[6,6]{0,1:T(8,128)S(1)} %fusion.42, f32[6]{0:T(128)S(1)} %multiply_subtract_fusion), channel_id=1, replica_groups=mesh['row'=4,'col'=8] {'row','col'}, use_global_device_ids=true, to_apply=%region_11.13 | all-reduce | flops 42 | bytes 336 | tf_op jit(solution)/shard_map/psum | solution.py:134
  (190 shorter events, 65.4 us)
Async XLA Ops:
  7.2 15.1 %copy-start.36 = (s32[1,128]{1,0:T(1,128)S(1)}, s32[1,128]{1,0:T(1,128)}, u32[]{:S(2)}) copy-start(s32[1,128]{1,0:T(1,128)} %param.16) | copy-start | bytes 1540
  7.2 411.4 %all-gather.2.cloned.1.call-start = ((), (), s32[]{:S(2)}) async-start(), calls=%async_computation | async-start | bytes 1081344 | tf_op jit(solution)/shard_map/all_gather | solution.py:116
  8.0 27.8 %collective-permute-start.6 = (f32[4,128]{0,1:T(8,128)S(1)}, f32[4,128]{0,1:T(8,128)S(1)}, u32[]{:S(2)}, u32[]{:S(2)}) collective-permute-start(f32[4,128]{0,1:T(8,128)S(1)} %copy.33), channel_id=1, source_target_pairs={{7,0},{0,1},{1,2},{2,3},{3,4},{4,5},{5,6},{6,7},{15,8},{8,9},{9,10... | collective-permute-start | bytes 6152 | tf_op jit(solution)/shard_map/ppermute | solution.py:22
  9.6 26.9 %collective-permute-start.5 = (f32[4,128]{0,1:T(8,128)S(1)}, f32[4,128]{0,1:T(8,128)S(1)}, u32[]{:S(2)}, u32[]{:S(2)}) collective-permute-start(f32[4,128]{0,1:T(8,128)S(1)} %copy.33), channel_id=1, source_target_pairs={{0,8},{8,16},{16,24},{1,9},{9,17},{17,25},{2,10},{10,18},{18,26},{... | collective-permute-start | bytes 6152 | tf_op jit(solution)/shard_map/ppermute | solution.py:16
  13.3 402.4 %collective-permute-start.8 = (f32[512,128]{0,1:T(8,128)}, f32[512,128]{0,1:T(8,128)}, u32[]{:S(2)}, u32[]{:S(2)}) collective-permute-start(f32[512,128]{0,1:T(8,128)} %copy.50), channel_id=1, source_target_pairs={{7,0},{0,1},{1,2},{2,3},{3,4},{4,5},{5,6},{6,7},{15,8},{8,9},{9,10... | collective-permute-start | bytes 786440 | tf_op jit(solution)/shard_map/ppermute | solution.py:22
  14.8 402.8 %collective-permute-start.7 = (f32[512,128]{0,1:T(8,128)}, f32[512,128]{0,1:T(8,128)S(1)}, u32[]{:S(2)}, u32[]{:S(2)}) collective-permute-start(f32[512,128]{0,1:T(8,128)} %copy.50), channel_id=1, source_target_pairs={{0,8},{8,16},{16,24},{1,9},{9,17},{17,25},{2,10},{10,18},{18,26},{... | collective-permute-start | bytes 786440 | tf_op jit(solution)/shard_map/ppermute | solution.py:16
  16.7 7.6 %collective-permute-start = (f32[4,16]{1,0:T(4,128)}, f32[4,16]{1,0:T(4,128)S(1)}, u32[]{:S(2)}, u32[]{:S(2)}) collective-permute-start(f32[4,16]{1,0:T(4,128)} %param.14), channel_id=1, source_target_pairs={{0,31},{1,0},{2,1},{3,2},{4,3},{5,4},{6,5},{7,6},{8,7},{9,8},{10,9... | collective-permute-start | bytes 776 | tf_op jit(solution)/shard_map/ppermute | solution.py:110
  17.4 16.3 %copy-start.14 = (pred[640,640]{1,0:T(32,128)(4,1)}, pred[640,640]{1,0:T(32,128)(4,1)S(1)}, u32[]{:S(2)}) copy-start(pred[640,640]{1,0:T(32,128)(4,1)S(1)} %iota_compare_fusion.1) | copy-start | bytes 1228804
  19.5 4.8 copy-start.25
  20.8 14.2 %copy-start.37 = (s32[1,384]{1,0:T(1,128)S(1)}, s32[1,384]{1,0:T(1,128)}, u32[]{:S(2)}) copy-start(s32[1,384]{1,0:T(1,128)} %param.17) | copy-start | bytes 4612
  20.8 20.5 %copy-start.27 = (f32[4,128]{1,0:T(4,128)S(1)}, f32[4,128]{1,0:T(4,128)}, u32[]{:S(2)}) copy-start(f32[4,128]{1,0:T(4,128)} %param.12) | copy-start | bytes 6148
  22.4 19.7 %copy-start.32 = (pred[64]{0:T(512)(128)(4,1)}, pred[64]{0:T(512)(128)(4,1)S(1)}, u32[]{:S(2)}) copy-start(pred[64]{0:T(512)(128)(4,1)S(1)} %get-tuple-element.22) | copy-start | bytes 196
  22.4 19.7 %copy-start.34 = (pred[64]{0:T(512)(128)(4,1)}, pred[64]{0:T(512)(128)(4,1)S(1)}, u32[]{:S(2)}) copy-start(pred[64]{0:T(512)(128)(4,1)S(1)} %get-tuple-element.50) | copy-start | bytes 196
  24.3 21.0 %copy-start.30 = (s32[1024]{0:T(1024)}, s32[1024]{0:T(1024)S(1)}, u32[]{:S(2)}) copy-start(s32[1024]{0:T(1024)S(1)} %pad_clamp_fusion) | copy-start | bytes 12292
  24.4 3.6 collective-permute-start.1
  24.9 20.5 %copy-start.31 = (s32[1024]{0:T(1024)}, s32[1024]{0:T(1024)S(1)}, u32[]{:S(2)}) copy-start(s32[1024]{0:T(1024)S(1)} %pad_clamp_fusion.1) | copy-start | bytes 12292
  28.1 5.6 %collective-permute-start.2 = (f32[4,64]{1,0:T(4,128)S(1)}, f32[4,64]{1,0:T(4,128)S(1)}, u32[]{:S(2)}, u32[]{:S(2)}) collective-permute-start(f32[4,64]{1,0:T(4,128)S(1)} %pad_maximum_fusion.15), channel_id=1, source_target_pairs={{0,28},{1,29},{2,30},{3,31},{4,0},{5,1},{6,2},{7,3},{8,4},{9,5},{1... | collective-permute-start | bytes 3080 | tf_op jit(solution)/shard_map/ppermute | solution.py:110
  33.7 3.4 collective-permute-start.3
  35.1 10.3 %copy-start.28 = (s32[384]{0:T(512)}, s32[384]{0:T(512)S(1)}, u32[]{:S(2)}) copy-start(s32[384]{0:T(512)S(1)} %reduce.36) | copy-start | bytes 4612
  37.2 3.6 collective-permute-start.4
  54.1 3.2 copy-start.26
  59.7 1.2 copy-start.9
  60.8 25.2 %copy-start.10 = (f32[640,640]{1,0:T(8,128)S(1)}, f32[640,640]{1,0:T(8,128)}, u32[]{:S(2)}) copy-start(f32[640,640]{1,0:T(8,128)} %copy-done.9) | copy-start | bytes 4915204
  87.6 0.7 copy-start.19
  117.3 0.7 copy-start.20
  211.9 1.2 copy-start.11
  211.9 56.1 %copy-start.8 = (f32[640,640]{1,0:T(8,128)S(1)}, f32[640,640]{1,0:T(8,128)}, u32[]{:S(2)}) copy-start(f32[640,640]{1,0:T(8,128)} %fusion.53) | copy-start | bytes 4915204
  265.2 4.4 copy-start.23
  268.0 6.5 %copy-start.6 = (f32[128,640]{1,0:T(8,128)}, f32[128,640]{1,0:T(8,128)S(1)}, u32[]{:S(2)}) copy-start(f32[128,640]{1,0:T(8,128)S(1)} %get-tuple-element.57) | copy-start | bytes 983044
  270.1 4.4 copy-start.12
  272.5 5.0 copy-start.15
  277.9 6.2 %copy-start.1 = (f32[640,640]{1,0:T(8,128)}, f32[640,640]{1,0:T(8,128)S(1)}, u32[]{:S(2)}) copy-start(f32[640,640]{1,0:T(8,128)S(1)} %convolution_dynamic-update-slice_fusion) | copy-start | bytes 4915204
  277.9 6.2 %copy-start.3 = (f32[640,640]{0,1:T(8,128)S(1)}, f32[640,640]{0,1:T(8,128)}, u32[]{:S(2)}) copy-start(f32[640,640]{0,1:T(8,128)} %get-tuple-element.30) | copy-start | bytes 4915204
  288.0 2.9 copy-start.4
  288.0 2.9 copy-start.22
  321.8 14.5 %copy-start.17 = (pred[512,512]{0,1:T(8,128)(4,1)S(1)}, pred[512,512]{0,1:T(8,128)(4,1)}, u32[]{:S(2)}) copy-start(pred[512,512]{0,1:T(8,128)(4,1)} %iota_compare_fusion.4) | copy-start | bytes 786436
  321.8 14.5 %copy-start.18 = (f32[512,512,1]{1,0,2:T(8,128)S(1)}, f32[512,512,1]{1,0,2:T(8,128)}, u32[]{:S(2)}) copy-start(f32[512,512,1]{1,0,2:T(8,128)} %convolution_bitcast_fusion.1) | copy-start | bytes 3145732
  352.3 44.5 %slice-start = ((s8[6291456]{0:T(1024)(128)(4,1)}), s8[2097152]{0:T(1024)(128)(4,1)S(1)}, s32[]{:S(2)}) async-start(s8[6291456]{0:T(1024)(128)(4,1)} %bitcast.147), calls=%async_computation.1 | async-start | bytes 4194304
  362.0 34.8 %slice-start.1 = ((s8[6291456]{0:T(1024)(128)(4,1)}), s8[4194304]{0:T(1024)(128)(4,1)S(1)}, s32[]{:S(2)}) async-start(s8[6291456]{0:T(1024)(128)(4,1)} %bitcast.147), calls=%async_computation.2 | async-start | bytes 8388608
  362.0 34.8 %copy-start = (f32[6,512,512]{2,0,1:T(8,128)S(1)}, f32[6,512,512]{2,0,1:T(8,128)}, u32[]{:S(2)}) copy-start(f32[6,512,512]{2,0,1:T(8,128)} %copy.44) | copy-start | bytes 18874372
  417.5 0.8 copy-start.35
  417.5 0.9 copy-start.33
  417.5 1.0 copy-start.29
  418.4 2.5 copy-start.2
  428.3 4.8 copy-start.7
  428.3 4.8 copy-start.13
  428.3 4.8 copy-start.16
  436.2 2.9 copy-start.5
  (3 other events, 2.0 us)
Sparse Core Ops, SparseCore 0:
  17.4 54.4 all-gather.1
